TPU v7x, 32 devices: a whole 2x2x4 slice. The times are simulated.
32 devices in a mesh: ens: 2 (over x), tile: 16 (over z, y, core).
Axes of the slice: x: 2, y: 2, z: 4, core: 2. Of those that a mesh axis runs over, the one named last changes fastest.
Arguments:
- final_adjoint: float32 [320, 32, 1024], P('ens', 'tile'), parts along dimension 0, may hold values from -0.5 to 1.5
- first_density: float32 [320, 32, 1024], P('ens', 'tile'), parts along dimension 0, may hold values from 0.05 to 2
- second_density: float32 [320, 32, 1024], P('ens', 'tile'), parts along dimension 0, may hold values from 0.05 to 2
- forage: float32 [4, 6, 32, 1024], P('ens', None, 'tile'), parts along dimension 0, may hold values from 5 to 50
- preference: float32 [32, 6], P('ens'), parts along dimension 0, may hold values from 0.02 to 0.3
- base_mortality: float32 [160], replicated, may hold values from 0.01 to 0.5
- age_class: int32 [160], replicated, may hold values from 0 to 15, never falling along the last dimension, each value on 1 to 20 neighbouring positions
- land_mask: int32 [32, 1024], P('tile'), may hold values 0 or 1
- east_velocity: float32 [32, 1024], P('tile'), may hold values from -0.1 to 0.1
- north_velocity: float32 [32, 1024], P('tile'), may hold values from -0.1 to 0.1
Outputs:
- initial_adjoint: float32 [320, 32, 1024], P('ens', 'tile'), parts along dimension 0
- forage_sensitivity: float32 [4, 6, 32, 1024], P('ens', None, 'tile'), parts along dimension 0
- preference_gradient: float32 [32, 6], P('ens'), parts along dimension 0
There are 2 independent parts, one for each index of `ens`. A program takes and returns all parts, laid end to end along the dimension named above; an argument that names none is the same for every part. Nothing has to cross between parts.
Inputs may be any that keep to these rules, and one draw needn't show every extreme that they name: `age_class`: never falls along the cohorts; every class holds 1 to 20 cohorts, one exactly that many.
All inputs are finite; a program needn't handle non-finite values. No bound on the sum of `land_mask` on one device may be relied on, other than what follows from the above.
Results may differ from a plain program's by a relative error of at most 0.00011.
Values sent between devices are 32-bit elements; how exact they have to be, the bound alone decides.
A program may use at most 64 MiB of HBM per device.

v0:
```python
import jax
import jax.numpy as jnp
from jax import lax
from jax.sharding import PartitionSpec as P

SUBSTEPS = 4
HIGH = lax.Precision.HIGHEST


def with_halo(cells, sides, width):
    for axis, dim in sides:
        count = lax.axis_size(axis)
        ends = count - 1
        head = lax.slice_in_dim(cells, 0, width, axis=dim)
        tail = lax.slice_in_dim(cells, cells.shape[dim] - width, cells.shape[dim], axis=dim)
        cells = jnp.concatenate(
            [
                lax.ppermute(tail, axis, [(i, (i + 1) % count) for i in range(ends)]),
                cells,
                lax.ppermute(head, axis, [((i + 1) % count, i) for i in range(ends)]),
            ],
            axis=dim,
        )
    return cells


def make_rates(extended):
    mask = extended[0]
    centre = mask[1:-1]
    east_velocity = extended[1][1:-1]
    north_velocity = extended[2][1:-1]
    rate_n = centre * mask[:-2] * (0.1 + jnp.maximum(north_velocity, 0.0))
    rate_s = centre * mask[2:] * (0.1 + jnp.maximum(-north_velocity, 0.0))
    rate_e = centre * jnp.roll(centre, -1, axis=1) * (0.1 + jnp.maximum(east_velocity, 0.0))
    rate_w = centre * jnp.roll(centre, 1, axis=1) * (0.1 + jnp.maximum(-east_velocity, 0.0))
    keep = 1.0 - rate_n - rate_s - rate_e - rate_w
    return (keep, rate_n, rate_s, rate_e, rate_w)


def transpose_step(padded, first_row, rates):
    count = padded.shape[1] - 2
    begin = first_row + 1
    keep, rate_n, rate_s, rate_e, rate_w = [r[begin : begin + count] for r in rates]
    centre = padded[:, 1:-1]
    return (
        keep * centre
        + rate_n * padded[:, :-2]
        + rate_s * padded[:, 2:]
        + rate_e * jnp.roll(centre, -1, axis=2)
        + rate_w * jnp.roll(centre, 1, axis=2)
    )


def transported(incoming, rates):
    carried = incoming

    def one_step(index, field):
        wide = with_halo(field, (("tile", 1),), 1)
        return transpose_step(wide, 0, rates)

    carried = lax.fori_loop(0, SUBSTEPS, one_step, carried)
    return carried


def month_adjoint(incoming, density, food, pref_rows, base_mortality, rates, onehot):
    carried = transported(incoming, rates)
    cohorts = carried.shape[0]
    aged = jnp.concatenate([carried[1:], carried[cohorts - 1 :]], axis=0).reshape(cohorts, -1)
    dens = density.reshape(cohorts, -1)
    feed = food.reshape(food.shape[0], -1)
    demand = jnp.dot(pref_rows.T, dens, precision=HIGH)
    total = feed + demand
    short = demand / total
    survival = jnp.exp(-(base_mortality[:, None] + jnp.dot(pref_rows, short, precision=HIGH)))
    grown = survival * dens
    adj_mort = -aged * grown
    adj_ratio = -jnp.dot(pref_rows.T, adj_mort, precision=HIGH)
    squared = total * total
    adj_demand = -adj_ratio * feed / squared
    sensitivity = adj_ratio * demand * feed / squared
    outgoing = aged * survival + jnp.dot(pref_rows, adj_demand, precision=HIGH)
    cohort_grad = jnp.dot(adj_mort, short.T, precision=HIGH) + jnp.dot(
        dens, adj_demand.T, precision=HIGH
    )
    class_grad = jnp.dot(onehot, cohort_grad, precision=HIGH)
    return (outgoing.reshape(density.shape), sensitivity.reshape(food.shape), class_grad)


def shards(
    final_adjoint,
    first_density,
    second_density,
    forage,
    preference,
    base_mortality,
    age_class,
    land_mask,
    east_velocity,
    north_velocity,
):
    classes = preference.shape[0]
    onehot = (age_class[None, :] == jnp.arange(classes, dtype=jnp.int32)[:, None]).astype(
        jnp.float32
    )
    pref_rows = jnp.dot(onehot.T, preference, precision=HIGH)
    fields = jnp.stack([land_mask.astype(jnp.float32), east_velocity, north_velocity], axis=0)
    extended = with_halo(fields, (("tile", 1),), 2)
    rates = make_rates(extended)
    cells = land_mask.shape[0] * lax.axis_size("tile") * land_mask.shape[1]
    middle, sens_two, grad_two = month_adjoint(
        final_adjoint, second_density, forage[1], pref_rows, base_mortality, rates, onehot
    )

    def month_total(local_grad):
        return lax.psum(local_grad, "tile")

    total_two = month_total(grad_two)
    initial, sens_one, grad_one = month_adjoint(
        middle, first_density, forage[0], pref_rows, base_mortality, rates, onehot
    )
    summed = month_total(grad_one) + total_two
    return (initial, jnp.stack([sens_one, sens_two], axis=0), summed / cells)


def solution(mesh):
    in_specs = (
        P("ens", "tile", None),
        P("ens", "tile", None),
        P("ens", "tile", None),
        P("ens", None, "tile", None),
        P("ens", None),
        P(),
        P(),
        P("tile", None),
        P("tile", None),
        P("tile", None),
    )
    out_specs = (P("ens", "tile", None), P("ens", None, "tile", None), P("ens", None))
    return jax.shard_map(shards, mesh=mesh, in_specs=in_specs, out_specs=out_specs, check_vma=False)
```

profile of v0, /device:TPU:0, one launch (start us, length us, event | category | flops | bytes accessed | tf_op | source)
XLA Modules:
  0.0 273.3 jit_solution(4688281940485553662)
XLA Ops:
  1.4 2.4 collective-permute-start.4
  8.8 2.4 fusion.15
  11.2 2.4 fusion.13
  14.5 94.6 %while.20 = (s32[]{:T(128)}, f32[160,2,1024]{2,1,0:T(2,128)S(1)}, f32[4,1024]{1,0:T(4,128)}, f32[4,1024]{1,0:T(4,128)}, f32[4,1024]{1,0:T(4,128)}, /*index=5*/f32[4,1024]{1,0:T(4,128)}, f32[4,1024]{1,0:T(4,128)}, s32[]{:T(128)}) while((s32[]{:T(128)}, f32[160,2,1024]{2,1,0:T(2,128)S(1)}, f32[4,1024]{1,0:T(4,128)}, f32[4,1024]{1,0:T(4,128)}, ...), condition=%wide.region_1.2_spmd, body=%wide.region_0.1_spmd.sunk | while | flops 4259842 | bytes 22864288 | solution.py:61
  17.4 6.6 %collective-permute-start.1 = (f32[160,1,1024]{2,1,0:T(1,128)S(1)}, f32[160,1,1024]{2,1,0:T(1,128)}, u32[]{:S(2)}, u32[]{:S(2)}) collective-permute-start(f32[160,1,1024]{2,1,0:T(1,128)S(1)} %get-tuple-element.228), channel_id=1, source_target_pairs={{0,1},{1,2},{2,3},{3,4},{4,5},{5,6},{6,7},{7,8},{8,9},{9,10},{10,1... | collective-permute-start | bytes 1966088 | tf_op jit(solution)/shard_map/while/body/eval_jaxpr/ppermute | solution.py:18
  26.7 1.8 fusion.74
  28.6 5.9 %fusion.75 = f32[160,2,1024]{2,1,0:T(2,128)S(1)} fusion(f32[160,1,1024]{2,1,0:T(1,128)S(1)} %collective-permute-done, f32[160,2,1024]{2,1,0:T(2,128)S(1)} %copy.37, f32[160,1,1024]{2,1,0:T(1,128)} %collective-permute-done.1, f32[160,2,1]{2,1,0:T(2,128)S(1)} %get-tuple-element.229, f32[160,2,1023]{2,1,0:T(2,128)S(1)} %get-tuple-element.230, ...), kind=kLoop, calls=%fused_computation.4.clone.1 | loop fusion | flops 4259840 | bytes 6594560 | tf_op jit(solution)/shard_map/while/body/eval_jaxpr/add | solution.py:46
  37.4 13.3 %collective-permute-start.1 = (f32[160,1,1024]{2,1,0:T(1,128)S(1)}, f32[160,1,1024]{2,1,0:T(1,128)}, u32[]{:S(2)}, u32[]{:S(2)}) collective-permute-start(f32[160,1,1024]{2,1,0:T(1,128)S(1)} %get-tuple-element.228), channel_id=1, source_target_pairs={{0,1},{1,2},{2,3},{3,4},{4,5},{5,6},{6,7},{7,8},{8,9},{9,10},{10,1... | collective-permute-start | bytes 1966088 | tf_op jit(solution)/shard_map/while/body/eval_jaxpr/ppermute | solution.py:18
  53.4 1.8 fusion.74
  55.2 5.9 %fusion.75 = f32[160,2,1024]{2,1,0:T(2,128)S(1)} fusion(f32[160,1,1024]{2,1,0:T(1,128)S(1)} %collective-permute-done, f32[160,2,1024]{2,1,0:T(2,128)S(1)} %copy.37, f32[160,1,1024]{2,1,0:T(1,128)} %collective-permute-done.1, f32[160,2,1]{2,1,0:T(2,128)S(1)} %get-tuple-element.229, f32[160,2,1023]{2,1,0:T(2,128)S(1)} %get-tuple-element.230, ...), kind=kLoop, calls=%fused_computation.4.clone.1 | loop fusion | flops 4259840 | bytes 6594560 | tf_op jit(solution)/shard_map/while/body/eval_jaxpr/add | solution.py:46
  64.0 9.1 %collective-permute-start.1 = (f32[160,1,1024]{2,1,0:T(1,128)S(1)}, f32[160,1,1024]{2,1,0:T(1,128)}, u32[]{:S(2)}, u32[]{:S(2)}) collective-permute-start(f32[160,1,1024]{2,1,0:T(1,128)S(1)} %get-tuple-element.228), channel_id=1, source_target_pairs={{0,1},{1,2},{2,3},{3,4},{4,5},{5,6},{6,7},{7,8},{8,9},{9,10},{10,1... | collective-permute-start | bytes 1966088 | tf_op jit(solution)/shard_map/while/body/eval_jaxpr/ppermute | solution.py:18
  75.8 1.8 fusion.74
  77.7 5.9 %fusion.75 = f32[160,2,1024]{2,1,0:T(2,128)S(1)} fusion(f32[160,1,1024]{2,1,0:T(1,128)S(1)} %collective-permute-done, f32[160,2,1024]{2,1,0:T(2,128)S(1)} %copy.37, f32[160,1,1024]{2,1,0:T(1,128)} %collective-permute-done.1, f32[160,2,1]{2,1,0:T(2,128)S(1)} %get-tuple-element.229, f32[160,2,1023]{2,1,0:T(2,128)S(1)} %get-tuple-element.230, ...), kind=kLoop, calls=%fused_computation.4.clone.1 | loop fusion | flops 4259840 | bytes 6594560 | tf_op jit(solution)/shard_map/while/body/eval_jaxpr/add | solution.py:46
  86.5 12.1 %collective-permute-start.1 = (f32[160,1,1024]{2,1,0:T(1,128)S(1)}, f32[160,1,1024]{2,1,0:T(1,128)}, u32[]{:S(2)}, u32[]{:S(2)}) collective-permute-start(f32[160,1,1024]{2,1,0:T(1,128)S(1)} %get-tuple-element.228), channel_id=1, source_target_pairs={{0,1},{1,2},{2,3},{3,4},{4,5},{5,6},{6,7},{7,8},{8,9},{9,10},{10,1... | collective-permute-start | bytes 1966088 | tf_op jit(solution)/shard_map/while/body/eval_jaxpr/ppermute | solution.py:18
  101.4 1.8 fusion.74
  103.2 5.9 %fusion.75 = f32[160,2,1024]{2,1,0:T(2,128)S(1)} fusion(f32[160,1,1024]{2,1,0:T(1,128)S(1)} %collective-permute-done, f32[160,2,1024]{2,1,0:T(2,128)S(1)} %copy.37, f32[160,1,1024]{2,1,0:T(1,128)} %collective-permute-done.1, f32[160,2,1]{2,1,0:T(2,128)S(1)} %get-tuple-element.229, f32[160,2,1023]{2,1,0:T(2,128)S(1)} %get-tuple-element.230, ...), kind=kLoop, calls=%fused_computation.4.clone.1 | loop fusion | flops 4259840 | bytes 6594560 | tf_op jit(solution)/shard_map/while/body/eval_jaxpr/add | solution.py:46
  111.9 1.8 fusion.31
  118.4 96.1 %while.21 = (s32[]{:T(128)}, f32[160,2,1024]{2,1,0:T(2,128)S(1)}, f32[4,1024]{1,0:T(4,128)}, f32[4,1024]{1,0:T(4,128)}, f32[4,1024]{1,0:T(4,128)}, /*index=5*/f32[4,1024]{1,0:T(4,128)}, f32[4,1024]{1,0:T(4,128)}, s32[]{:T(128)}) while((s32[]{:T(128)}, f32[160,2,1024]{2,1,0:T(2,128)S(1)}, f32[4,1024]{1,0:T(4,128)}, f32[4,1024]{1,0:T(4,128)}, ...), condition=%wide.region_3.4_spmd, body=%wide.region_2.3_spmd.sunk | while | flops 4259842 | bytes 22864288 | solution.py:61
  121.4 9.1 %collective-permute-start.3 = (f32[160,1,1024]{2,1,0:T(1,128)S(1)}, f32[160,1,1024]{2,1,0:T(1,128)}, u32[]{:S(2)}, u32[]{:S(2)}) collective-permute-start(f32[160,1,1024]{2,1,0:T(1,128)S(1)} %get-tuple-element.241), channel_id=1, source_target_pairs={{0,1},{1,2},{2,3},{3,4},{4,5},{5,6},{6,7},{7,8},{8,9},{9,10},{10,1... | collective-permute-start | bytes 1966088 | tf_op jit(solution)/shard_map/while/body/eval_jaxpr/ppermute | solution.py:18
  133.2 1.8 fusion.78
  135.1 5.9 %fusion.79 = f32[160,2,1024]{2,1,0:T(2,128)S(1)} fusion(f32[160,1,1024]{2,1,0:T(1,128)S(1)} %collective-permute-done.2, f32[160,2,1024]{2,1,0:T(2,128)S(1)} %copy.38, f32[160,1,1024]{2,1,0:T(1,128)} %collective-permute-done.3, f32[160,2,1]{2,1,0:T(2,128)S(1)} %get-tuple-element.242, f32[160,2,1023]{2,1,0:T(2,128)S(1)} %get-tuple-element.243, ...), kind=kLoop, calls=%fused_computation.14.clone.1 | loop fusion | flops 4259840 | bytes 6594560 | tf_op jit(solution)/shard_map/while/body/eval_jaxpr/add | solution.py:46
  143.9 12.2 %collective-permute-start.3 = (f32[160,1,1024]{2,1,0:T(1,128)S(1)}, f32[160,1,1024]{2,1,0:T(1,128)}, u32[]{:S(2)}, u32[]{:S(2)}) collective-permute-start(f32[160,1,1024]{2,1,0:T(1,128)S(1)} %get-tuple-element.241), channel_id=1, source_target_pairs={{0,1},{1,2},{2,3},{3,4},{4,5},{5,6},{6,7},{7,8},{8,9},{9,10},{10,1... | collective-permute-start | bytes 1966088 | tf_op jit(solution)/shard_map/while/body/eval_jaxpr/ppermute | solution.py:18
  158.7 1.8 fusion.78
  160.6 5.9 %fusion.79 = f32[160,2,1024]{2,1,0:T(2,128)S(1)} fusion(f32[160,1,1024]{2,1,0:T(1,128)S(1)} %collective-permute-done.2, f32[160,2,1024]{2,1,0:T(2,128)S(1)} %copy.38, f32[160,1,1024]{2,1,0:T(1,128)} %collective-permute-done.3, f32[160,2,1]{2,1,0:T(2,128)S(1)} %get-tuple-element.242, f32[160,2,1023]{2,1,0:T(2,128)S(1)} %get-tuple-element.243, ...), kind=kLoop, calls=%fused_computation.14.clone.1 | loop fusion | flops 4259840 | bytes 6594560 | tf_op jit(solution)/shard_map/while/body/eval_jaxpr/add | solution.py:46
  169.4 9.2 %collective-permute-start.3 = (f32[160,1,1024]{2,1,0:T(1,128)S(1)}, f32[160,1,1024]{2,1,0:T(1,128)}, u32[]{:S(2)}, u32[]{:S(2)}) collective-permute-start(f32[160,1,1024]{2,1,0:T(1,128)S(1)} %get-tuple-element.241), channel_id=1, source_target_pairs={{0,1},{1,2},{2,3},{3,4},{4,5},{5,6},{6,7},{7,8},{8,9},{9,10},{10,1... | collective-permute-start | bytes 1966088 | tf_op jit(solution)/shard_map/while/body/eval_jaxpr/ppermute | solution.py:18
  181.3 1.8 fusion.78
  183.1 5.9 %fusion.79 = f32[160,2,1024]{2,1,0:T(2,128)S(1)} fusion(f32[160,1,1024]{2,1,0:T(1,128)S(1)} %collective-permute-done.2, f32[160,2,1024]{2,1,0:T(2,128)S(1)} %copy.38, f32[160,1,1024]{2,1,0:T(1,128)} %collective-permute-done.3, f32[160,2,1]{2,1,0:T(2,128)S(1)} %get-tuple-element.242, f32[160,2,1023]{2,1,0:T(2,128)S(1)} %get-tuple-element.243, ...), kind=kLoop, calls=%fused_computation.14.clone.1 | loop fusion | flops 4259840 | bytes 6594560 | tf_op jit(solution)/shard_map/while/body/eval_jaxpr/add | solution.py:46
  191.9 12.1 %collective-permute-start.3 = (f32[160,1,1024]{2,1,0:T(1,128)S(1)}, f32[160,1,1024]{2,1,0:T(1,128)}, u32[]{:S(2)}, u32[]{:S(2)}) collective-permute-start(f32[160,1,1024]{2,1,0:T(1,128)S(1)} %get-tuple-element.241), channel_id=1, source_target_pairs={{0,1},{1,2},{2,3},{3,4},{4,5},{5,6},{6,7},{7,8},{8,9},{9,10},{10,1... | collective-permute-start | bytes 1966088 | tf_op jit(solution)/shard_map/while/body/eval_jaxpr/ppermute | solution.py:18
  206.7 1.8 fusion.78
  208.5 5.9 %fusion.79 = f32[160,2,1024]{2,1,0:T(2,128)S(1)} fusion(f32[160,1,1024]{2,1,0:T(1,128)S(1)} %collective-permute-done.2, f32[160,2,1024]{2,1,0:T(2,128)S(1)} %copy.38, f32[160,1,1024]{2,1,0:T(1,128)} %collective-permute-done.3, f32[160,2,1]{2,1,0:T(2,128)S(1)} %get-tuple-element.242, f32[160,2,1023]{2,1,0:T(2,128)S(1)} %get-tuple-element.243, ...), kind=kLoop, calls=%fused_computation.14.clone.1 | loop fusion | flops 4259840 | bytes 6594560 | tf_op jit(solution)/shard_map/while/body/eval_jaxpr/add | solution.py:46
  224.0 45.8 %psum.16 = f32[16,6]{0,1:T(8,128)S(1)} all-reduce(f32[16,6]{0,1:T(8,128)S(1)} %convolution_add_fusion.4), channel_id=1, replica_groups=mesh['ens'=2,'tile'=16] {'tile'}, use_global_device_ids=true, to_apply=%region_4.5 | all-reduce | flops 96 | bytes 768 | tf_op jit(solution)/shard_map/psum | solution.py:115
  270.4 2.2 reshape.64
  (319 shorter events, 68.1 us)
Async XLA Ops:
  1.4 12.2 %collective-permute-start.4 = (f32[3,2,1024]{2,1,0:T(2,128)S(1)}, f32[3,2,1024]{2,1,0:T(2,128)S(1)}, u32[]{:S(2)}, u32[]{:S(2)}) collective-permute-start(f32[3,2,1024]{2,1,0:T(2,128)S(1)} %pad_maximum_fusion.7), channel_id=1, source_target_pairs={{0,1},{1,2},{2,3},{3,4},{4,5},{5,6},{6,7},{7,8},{8,9},{9,10},{10,1... | collective-permute-start | bytes 73736 | tf_op jit(solution)/shard_map/ppermute | solution.py:18
  3.8 9.8 %collective-permute-start.5 = (f32[3,2,1024]{2,1,0:T(2,128)S(1)}, f32[3,2,1024]{2,1,0:T(2,128)S(1)}, u32[]{:S(2)}, u32[]{:S(2)}) collective-permute-start(f32[3,2,1024]{2,1,0:T(2,128)S(1)} %pad_maximum_fusion.7), channel_id=1, source_target_pairs={{1,0},{2,1},{3,2},{4,3},{5,4},{6,5},{7,6},{8,7},{9,8},{10,9},{11,1... | collective-permute-start | bytes 73736 | tf_op jit(solution)/shard_map/ppermute | solution.py:20
  16.1 12.4 %collective-permute-start = (f32[160,1,1024]{2,1,0:T(1,128)S(1)}, f32[160,1,1024]{2,1,0:T(1,128)S(1)}, u32[]{:S(2)}, u32[]{:S(2)}) collective-permute-start(f32[160,1,1024]{2,1,0:T(1,128)S(1)} %get-tuple-element.227), channel_id=1, source_target_pairs={{1,0},{2,1},{3,2},{4,3},{5,4},{6,5},{7,6},{8,7},{9,8},{10,9},{11,1... | collective-permute-start | bytes 1966088 | tf_op jit(solution)/shard_map/while/body/eval_jaxpr/ppermute | solution.py:20
  17.4 11.2 %collective-permute-start.1 = (f32[160,1,1024]{2,1,0:T(1,128)S(1)}, f32[160,1,1024]{2,1,0:T(1,128)}, u32[]{:S(2)}, u32[]{:S(2)}) collective-permute-start(f32[160,1,1024]{2,1,0:T(1,128)S(1)} %get-tuple-element.228), channel_id=1, source_target_pairs={{0,1},{1,2},{2,3},{3,4},{4,5},{5,6},{6,7},{7,8},{8,9},{9,10},{10,1... | collective-permute-start | bytes 1966088 | tf_op jit(solution)/shard_map/while/body/eval_jaxpr/ppermute | solution.py:18
  35.0 15.7 %copy-start.32 = (f32[4,1024]{1,0:T(4,128)S(1)}, f32[4,1024]{1,0:T(4,128)}, u32[]{:S(2)}) copy-start(f32[4,1024]{1,0:T(4,128)} %get-tuple-element.268) | copy-start | bytes 49156 | tf_op jit(solution)/shard_map/while
  35.0 15.7 %copy-start.30 = (f32[4,1024]{1,0:T(4,128)S(1)}, f32[4,1024]{1,0:T(4,128)}, u32[]{:S(2)}) copy-start(f32[4,1024]{1,0:T(4,128)} %get-tuple-element.267) | copy-start | bytes 49156 | tf_op jit(solution)/shard_map/while
  35.0 16.3 %copy-start.28 = (f32[4,1024]{1,0:T(4,128)S(1)}, f32[4,1024]{1,0:T(4,128)}, u32[]{:S(2)}) copy-start(f32[4,1024]{1,0:T(4,128)} %get-tuple-element.266) | copy-start | bytes 49156 | tf_op jit(solution)/shard_map/while
  35.0 16.9 %copy-start.26 = (f32[4,1024]{1,0:T(4,128)S(1)}, f32[4,1024]{1,0:T(4,128)}, u32[]{:S(2)}) copy-start(f32[4,1024]{1,0:T(4,128)} %get-tuple-element.265) | copy-start | bytes 49156 | tf_op jit(solution)/shard_map/while
  35.0 17.5 %copy-start.24 = (f32[4,1024]{1,0:T(4,128)S(1)}, f32[4,1024]{1,0:T(4,128)}, u32[]{:S(2)}) copy-start(f32[4,1024]{1,0:T(4,128)} %get-tuple-element.264) | copy-start | bytes 49156 | tf_op jit(solution)/shard_map/while
  36.1 19.1 %collective-permute-start = (f32[160,1,1024]{2,1,0:T(1,128)S(1)}, f32[160,1,1024]{2,1,0:T(1,128)S(1)}, u32[]{:S(2)}, u32[]{:S(2)}) collective-permute-start(f32[160,1,1024]{2,1,0:T(1,128)S(1)} %get-tuple-element.227), channel_id=1, source_target_pairs={{1,0},{2,1},{3,2},{4,3},{5,4},{6,5},{7,6},{8,7},{9,8},{10,9},{11,1... | collective-permute-start | bytes 1966088 | tf_op jit(solution)/shard_map/while/body/eval_jaxpr/ppermute | solution.py:20
  37.4 17.8 %collective-permute-start.1 = (f32[160,1,1024]{2,1,0:T(1,128)S(1)}, f32[160,1,1024]{2,1,0:T(1,128)}, u32[]{:S(2)}, u32[]{:S(2)}) collective-permute-start(f32[160,1,1024]{2,1,0:T(1,128)S(1)} %get-tuple-element.228), channel_id=1, source_target_pairs={{0,1},{1,2},{2,3},{3,4},{4,5},{5,6},{6,7},{7,8},{8,9},{9,10},{10,1... | collective-permute-start | bytes 1966088 | tf_op jit(solution)/shard_map/while/body/eval_jaxpr/ppermute | solution.py:18
  62.7 14.9 %collective-permute-start = (f32[160,1,1024]{2,1,0:T(1,128)S(1)}, f32[160,1,1024]{2,1,0:T(1,128)S(1)}, u32[]{:S(2)}, u32[]{:S(2)}) collective-permute-start(f32[160,1,1024]{2,1,0:T(1,128)S(1)} %get-tuple-element.227), channel_id=1, source_target_pairs={{1,0},{2,1},{3,2},{4,3},{5,4},{6,5},{7,6},{8,7},{9,8},{10,9},{11,1... | collective-permute-start | bytes 1966088 | tf_op jit(solution)/shard_map/while/body/eval_jaxpr/ppermute | solution.py:20
  64.0 13.6 %collective-permute-start.1 = (f32[160,1,1024]{2,1,0:T(1,128)S(1)}, f32[160,1,1024]{2,1,0:T(1,128)}, u32[]{:S(2)}, u32[]{:S(2)}) collective-permute-start(f32[160,1,1024]{2,1,0:T(1,128)S(1)} %get-tuple-element.228), channel_id=1, source_target_pairs={{0,1},{1,2},{2,3},{3,4},{4,5},{5,6},{6,7},{7,8},{8,9},{9,10},{10,1... | collective-permute-start | bytes 1966088 | tf_op jit(solution)/shard_map/while/body/eval_jaxpr/ppermute | solution.py:18
  84.2 15.1 %copy-start.28 = (f32[4,1024]{1,0:T(4,128)S(1)}, f32[4,1024]{1,0:T(4,128)}, u32[]{:S(2)}) copy-start(f32[4,1024]{1,0:T(4,128)} %get-tuple-element.266) | copy-start | bytes 49156 | tf_op jit(solution)/shard_map/while
  84.2 15.7 %copy-start.26 = (f32[4,1024]{1,0:T(4,128)S(1)}, f32[4,1024]{1,0:T(4,128)}, u32[]{:S(2)}) copy-start(f32[4,1024]{1,0:T(4,128)} %get-tuple-element.265) | copy-start | bytes 49156 | tf_op jit(solution)/shard_map/while
  84.2 16.3 %copy-start.24 = (f32[4,1024]{1,0:T(4,128)S(1)}, f32[4,1024]{1,0:T(4,128)}, u32[]{:S(2)}) copy-start(f32[4,1024]{1,0:T(4,128)} %get-tuple-element.264) | copy-start | bytes 49156 | tf_op jit(solution)/shard_map/while
  85.2 17.9 %collective-permute-start = (f32[160,1,1024]{2,1,0:T(1,128)S(1)}, f32[160,1,1024]{2,1,0:T(1,128)S(1)}, u32[]{:S(2)}, u32[]{:S(2)}) collective-permute-start(f32[160,1,1024]{2,1,0:T(1,128)S(1)} %get-tuple-element.227), channel_id=1, source_target_pairs={{1,0},{2,1},{3,2},{4,3},{5,4},{6,5},{7,6},{8,7},{9,8},{10,9},{11,1... | collective-permute-start | bytes 1966088 | tf_op jit(solution)/shard_map/while/body/eval_jaxpr/ppermute | solution.py:20
  86.5 16.7 %collective-permute-start.1 = (f32[160,1,1024]{2,1,0:T(1,128)S(1)}, f32[160,1,1024]{2,1,0:T(1,128)}, u32[]{:S(2)}, u32[]{:S(2)}) collective-permute-start(f32[160,1,1024]{2,1,0:T(1,128)S(1)} %get-tuple-element.228), channel_id=1, source_target_pairs={{0,1},{1,2},{2,3},{3,4},{4,5},{5,6},{6,7},{7,8},{8,9},{9,10},{10,1... | collective-permute-start | bytes 1966088 | tf_op jit(solution)/shard_map/while/body/eval_jaxpr/ppermute | solution.py:18
  120.1 14.9 %collective-permute-start.2 = (f32[160,1,1024]{2,1,0:T(1,128)S(1)}, f32[160,1,1024]{2,1,0:T(1,128)S(1)}, u32[]{:S(2)}, u32[]{:S(2)}) collective-permute-start(f32[160,1,1024]{2,1,0:T(1,128)S(1)} %get-tuple-element.240), channel_id=1, source_target_pairs={{1,0},{2,1},{3,2},{4,3},{5,4},{6,5},{7,6},{8,7},{9,8},{10,9},{11,1... | collective-permute-start | bytes 1966088 | tf_op jit(solution)/shard_map/while/body/eval_jaxpr/ppermute | solution.py:20
  121.4 13.6 %collective-permute-start.3 = (f32[160,1,1024]{2,1,0:T(1,128)S(1)}, f32[160,1,1024]{2,1,0:T(1,128)}, u32[]{:S(2)}, u32[]{:S(2)}) collective-permute-start(f32[160,1,1024]{2,1,0:T(1,128)S(1)} %get-tuple-element.241), channel_id=1, source_target_pairs={{0,1},{1,2},{2,3},{3,4},{4,5},{5,6},{6,7},{7,8},{8,9},{9,10},{10,1... | collective-permute-start | bytes 1966088 | tf_op jit(solution)/shard_map/while/body/eval_jaxpr/ppermute | solution.py:18
  141.5 15.1 %copy-start.29 = (f32[4,1024]{1,0:T(4,128)S(1)}, f32[4,1024]{1,0:T(4,128)}, u32[]{:S(2)}) copy-start(f32[4,1024]{1,0:T(4,128)} %get-tuple-element.290) | copy-start | bytes 49156 | tf_op jit(solution)/shard_map/while
  141.5 15.7 %copy-start.27 = (f32[4,1024]{1,0:T(4,128)S(1)}, f32[4,1024]{1,0:T(4,128)}, u32[]{:S(2)}) copy-start(f32[4,1024]{1,0:T(4,128)} %get-tuple-element.289) | copy-start | bytes 49156 | tf_op jit(solution)/shard_map/while
  141.5 16.3 %copy-start.25 = (f32[4,1024]{1,0:T(4,128)S(1)}, f32[4,1024]{1,0:T(4,128)}, u32[]{:S(2)}) copy-start(f32[4,1024]{1,0:T(4,128)} %get-tuple-element.288) | copy-start | bytes 49156 | tf_op jit(solution)/shard_map/while
  142.6 17.9 %collective-permute-start.2 = (f32[160,1,1024]{2,1,0:T(1,128)S(1)}, f32[160,1,1024]{2,1,0:T(1,128)S(1)}, u32[]{:S(2)}, u32[]{:S(2)}) collective-permute-start(f32[160,1,1024]{2,1,0:T(1,128)S(1)} %get-tuple-element.240), channel_id=1, source_target_pairs={{1,0},{2,1},{3,2},{4,3},{5,4},{6,5},{7,6},{8,7},{9,8},{10,9},{11,1... | collective-permute-start | bytes 1966088 | tf_op jit(solution)/shard_map/while/body/eval_jaxpr/ppermute | solution.py:20
  143.9 16.7 %collective-permute-start.3 = (f32[160,1,1024]{2,1,0:T(1,128)S(1)}, f32[160,1,1024]{2,1,0:T(1,128)}, u32[]{:S(2)}, u32[]{:S(2)}) collective-permute-start(f32[160,1,1024]{2,1,0:T(1,128)S(1)} %get-tuple-element.241), channel_id=1, source_target_pairs={{0,1},{1,2},{2,3},{3,4},{4,5},{5,6},{6,7},{7,8},{8,9},{9,10},{10,1... | collective-permute-start | bytes 1966088 | tf_op jit(solution)/shard_map/while/body/eval_jaxpr/ppermute | solution.py:18
  168.1 15.0 %collective-permute-start.2 = (f32[160,1,1024]{2,1,0:T(1,128)S(1)}, f32[160,1,1024]{2,1,0:T(1,128)S(1)}, u32[]{:S(2)}, u32[]{:S(2)}) collective-permute-start(f32[160,1,1024]{2,1,0:T(1,128)S(1)} %get-tuple-element.240), channel_id=1, source_target_pairs={{1,0},{2,1},{3,2},{4,3},{5,4},{6,5},{7,6},{8,7},{9,8},{10,9},{11,1... | collective-permute-start | bytes 1966088 | tf_op jit(solution)/shard_map/while/body/eval_jaxpr/ppermute | solution.py:20
  169.4 13.7 %collective-permute-start.3 = (f32[160,1,1024]{2,1,0:T(1,128)S(1)}, f32[160,1,1024]{2,1,0:T(1,128)}, u32[]{:S(2)}, u32[]{:S(2)}) collective-permute-start(f32[160,1,1024]{2,1,0:T(1,128)S(1)} %get-tuple-element.241), channel_id=1, source_target_pairs={{0,1},{1,2},{2,3},{3,4},{4,5},{5,6},{6,7},{7,8},{8,9},{9,10},{10,1... | collective-permute-start | bytes 1966088 | tf_op jit(solution)/shard_map/while/body/eval_jaxpr/ppermute | solution.py:18
  189.6 15.6 %copy-start.27 = (f32[4,1024]{1,0:T(4,128)S(1)}, f32[4,1024]{1,0:T(4,128)}, u32[]{:S(2)}) copy-start(f32[4,1024]{1,0:T(4,128)} %get-tuple-element.289) | copy-start | bytes 49156 | tf_op jit(solution)/shard_map/while
  189.6 16.2 %copy-start.25 = (f32[4,1024]{1,0:T(4,128)S(1)}, f32[4,1024]{1,0:T(4,128)}, u32[]{:S(2)}) copy-start(f32[4,1024]{1,0:T(4,128)} %get-tuple-element.288) | copy-start | bytes 49156 | tf_op jit(solution)/shard_map/while
  190.6 17.8 %collective-permute-start.2 = (f32[160,1,1024]{2,1,0:T(1,128)S(1)}, f32[160,1,1024]{2,1,0:T(1,128)S(1)}, u32[]{:S(2)}, u32[]{:S(2)}) collective-permute-start(f32[160,1,1024]{2,1,0:T(1,128)S(1)} %get-tuple-element.240), channel_id=1, source_target_pairs={{1,0},{2,1},{3,2},{4,3},{5,4},{6,5},{7,6},{8,7},{9,8},{10,9},{11,1... | collective-permute-start | bytes 1966088 | tf_op jit(solution)/shard_map/while/body/eval_jaxpr/ppermute | solution.py:20
  191.9 16.6 %collective-permute-start.3 = (f32[160,1,1024]{2,1,0:T(1,128)S(1)}, f32[160,1,1024]{2,1,0:T(1,128)}, u32[]{:S(2)}, u32[]{:S(2)}) collective-permute-start(f32[160,1,1024]{2,1,0:T(1,128)S(1)} %get-tuple-element.241), channel_id=1, source_target_pairs={{0,1},{1,2},{2,3},{3,4},{4,5},{5,6},{6,7},{7,8},{8,9},{9,10},{10,1... | collective-permute-start | bytes 1966088 | tf_op jit(solution)/shard_map/while/body/eval_jaxpr/ppermute | solution.py:18
  222.3 48.1 %copy-start.35 = (f32[6,2048]{1,0:T(8,128)S(1)}, f32[6,2048]{1,0:T(8,128)}, u32[]{:S(2)}) copy-start(f32[6,2048]{1,0:T(8,128)} %get-tuple-element.132) | copy-start | bytes 147460
  (82 other events, 436.9 us)
where the time goes:
time: 274 us; the launch traced here: 273 us
  starting transfers between devices  97.7 us (36%)
  local copies, waits for them, and re-layouts  59.1 us (22%)
  other arithmetic  50.8 us (19%)
  blocking collectives  45.8 us (17%)
  matrix products  17.2 us (6%)
    ppermute x9, starting transfers between devices, with_halo(): lax.ppermute(tail, axis, [(i, (i + 1) % count) for i in range(ends)])  86.1 us
    add x8, other arithmetic, transpose_step(): keep * centre + rate_n * padded[:, :-2] + rate_s * padded[:, 2:]  47.6 us
    psum x1, blocking collectives, month_total(): return lax.psum(local_grad, 'tile')  45.8 us
    slice x40, local copies, waits for them, and re-layouts, transpose_step(): r[begin:begin + count]  19.3 us
    slice x16, local copies, waits for them, and re-layouts, transpose_step(): jnp.roll(centre, 1, axis=2)  16.1 us
    ppermute x9, starting transfers between devices, with_halo(): lax.ppermute(head, axis, [((i + 1) % count, i) for i in range(ends)])  11.6 us
    slice x8, local copies, waits for them, and re-layouts, with_halo(): lax.slice_in_dim(cells, cells.shape[dim] - width, cells.shape[dim], axis=...  8.1 us
    unnamed x55, local copies, waits for them, and re-layouts  7.25 us
  transfers between devices with their start and end apart: 18, of which 0 were waited for; matrix products, arithmetic and copies ran while one was open for 16% of the time, Pallas kernels for 0%

commit v1 on v0

--- a/solution.py
+++ b/solution.py
@@ -112,7 +112,7 @@
     )
 
     def month_total(local_grad):
-        return lax.psum(local_grad, "tile")
+        return jnp.sum(lax.all_gather(local_grad, "tile"), axis=0)
 
     total_two = month_total(grad_two)
     initial, sens_one, grad_one = month_adjoint(

time: 274 us -> 283 us (1.033)
  blocking collectives: 45.8 us -> 54.4 us
    all_gather x0 -> x2, blocking collectives: none -> 54.4 us  [month_total(): return jnp.sum(lax.all_gather(local_grad, 'tile'), axis=0)]
    psum x1 -> x0, blocking collectives: 45.8 us -> none  [month_total(): return lax.psum(local_grad, 'tile')]
  transfers between devices with their start and end apart: 18 -> 18, of which waited for: 0 -> 0; matrix products, arithmetic and copies ran while one was open for 16% -> 15% of each run, Pallas kernels for 0% -> 0%
where the time goes in v1:
time: 283 us; the launch traced here: 282 us
  starting transfers between devices  97.7 us (35%)
  local copies, waits for them, and re-layouts  59.1 us (21%)
  blocking collectives  54.4 us (19%)
  other arithmetic  50.8 us (18%)
  matrix products  17.2 us (6%)
    ppermute x9, starting transfers between devices, with_halo(): lax.ppermute(tail, axis, [(i, (i + 1) % count) for i in range(ends)])  86.1 us
    all_gather x2, blocking collectives, month_total(): return jnp.sum(lax.all_gather(local_grad, 'tile'), axis=0)  54.4 us
    add x8, other arithmetic, transpose_step(): keep * centre + rate_n * padded[:, :-2] + rate_s * padded[:, 2:]  47.6 us
    slice x40, local copies, waits for them, and re-layouts, transpose_step(): r[begin:begin + count]  19.2 us
    slice x16, local copies, waits for them, and re-layouts, transpose_step(): jnp.roll(centre, 1, axis=2)  16.1 us
    ppermute x9, starting transfers between devices, with_halo(): lax.ppermute(head, axis, [((i + 1) % count, i) for i in range(ends)])  11.6 us
    slice x8, local copies, waits for them, and re-layouts, with_halo(): lax.slice_in_dim(cells, cells.shape[dim] - width, cells.shape[dim], axis=...  8.1 us
    unnamed x55, local copies, waits for them, and re-layouts  7.24 us
  transfers between devices with their start and end apart: 18, of which 0 were waited for; matrix products, arithmetic and copies ran while one was open for 15% of the time, Pallas kernels for 0%

profile of v1, /device:TPU:0, one launch (start us, length us, event | category | flops | bytes accessed | tf_op | source)
XLA Modules:
  0.0 282.0 jit_solution(13286658116738015424)
XLA Ops:
  1.4 2.4 collective-permute-start.4
  8.8 2.4 fusion.15
  11.2 2.4 fusion.13
  14.5 94.6 %while.20 = (s32[]{:T(128)}, f32[160,2,1024]{2,1,0:T(2,128)S(1)}, f32[4,1024]{1,0:T(4,128)}, f32[4,1024]{1,0:T(4,128)}, f32[4,1024]{1,0:T(4,128)}, /*index=5*/f32[4,1024]{1,0:T(4,128)}, f32[4,1024]{1,0:T(4,128)}, s32[]{:T(128)}) while((s32[]{:T(128)}, f32[160,2,1024]{2,1,0:T(2,128)S(1)}, f32[4,1024]{1,0:T(4,128)}, f32[4,1024]{1,0:T(4,128)}, ...), condition=%wide.region_1.2_spmd, body=%wide.region_0.1_spmd.sunk | while | flops 4259842 | bytes 22864288 | solution.py:61
  17.4 6.6 %collective-permute-start.1 = (f32[160,1,1024]{2,1,0:T(1,128)S(1)}, f32[160,1,1024]{2,1,0:T(1,128)}, u32[]{:S(2)}, u32[]{:S(2)}) collective-permute-start(f32[160,1,1024]{2,1,0:T(1,128)S(1)} %get-tuple-element.228), channel_id=1, source_target_pairs={{0,1},{1,2},{2,3},{3,4},{4,5},{5,6},{6,7},{7,8},{8,9},{9,10},{10,1... | collective-permute-start | bytes 1966088 | tf_op jit(solution)/shard_map/while/body/eval_jaxpr/ppermute | solution.py:18
  26.7 1.8 fusion.73
  28.6 5.9 %fusion.74 = f32[160,2,1024]{2,1,0:T(2,128)S(1)} fusion(f32[160,1,1024]{2,1,0:T(1,128)S(1)} %collective-permute-done, f32[160,2,1024]{2,1,0:T(2,128)S(1)} %copy.37, f32[160,1,1024]{2,1,0:T(1,128)} %collective-permute-done.1, f32[160,2,1]{2,1,0:T(2,128)S(1)} %get-tuple-element.229, f32[160,2,1023]{2,1,0:T(2,128)S(1)} %get-tuple-element.230, ...), kind=kLoop, calls=%fused_computation.4.clone.1 | loop fusion | flops 4259840 | bytes 6594560 | tf_op jit(solution)/shard_map/while/body/eval_jaxpr/add | solution.py:46
  37.4 13.3 %collective-permute-start.1 = (f32[160,1,1024]{2,1,0:T(1,128)S(1)}, f32[160,1,1024]{2,1,0:T(1,128)}, u32[]{:S(2)}, u32[]{:S(2)}) collective-permute-start(f32[160,1,1024]{2,1,0:T(1,128)S(1)} %get-tuple-element.228), channel_id=1, source_target_pairs={{0,1},{1,2},{2,3},{3,4},{4,5},{5,6},{6,7},{7,8},{8,9},{9,10},{10,1... | collective-permute-start | bytes 1966088 | tf_op jit(solution)/shard_map/while/body/eval_jaxpr/ppermute | solution.py:18
  53.4 1.8 fusion.73
  55.2 5.9 %fusion.74 = f32[160,2,1024]{2,1,0:T(2,128)S(1)} fusion(f32[160,1,1024]{2,1,0:T(1,128)S(1)} %collective-permute-done, f32[160,2,1024]{2,1,0:T(2,128)S(1)} %copy.37, f32[160,1,1024]{2,1,0:T(1,128)} %collective-permute-done.1, f32[160,2,1]{2,1,0:T(2,128)S(1)} %get-tuple-element.229, f32[160,2,1023]{2,1,0:T(2,128)S(1)} %get-tuple-element.230, ...), kind=kLoop, calls=%fused_computation.4.clone.1 | loop fusion | flops 4259840 | bytes 6594560 | tf_op jit(solution)/shard_map/while/body/eval_jaxpr/add | solution.py:46
  64.0 9.1 %collective-permute-start.1 = (f32[160,1,1024]{2,1,0:T(1,128)S(1)}, f32[160,1,1024]{2,1,0:T(1,128)}, u32[]{:S(2)}, u32[]{:S(2)}) collective-permute-start(f32[160,1,1024]{2,1,0:T(1,128)S(1)} %get-tuple-element.228), channel_id=1, source_target_pairs={{0,1},{1,2},{2,3},{3,4},{4,5},{5,6},{6,7},{7,8},{8,9},{9,10},{10,1... | collective-permute-start | bytes 1966088 | tf_op jit(solution)/shard_map/while/body/eval_jaxpr/ppermute | solution.py:18
  75.9 1.8 fusion.73
  77.7 5.9 %fusion.74 = f32[160,2,1024]{2,1,0:T(2,128)S(1)} fusion(f32[160,1,1024]{2,1,0:T(1,128)S(1)} %collective-permute-done, f32[160,2,1024]{2,1,0:T(2,128)S(1)} %copy.37, f32[160,1,1024]{2,1,0:T(1,128)} %collective-permute-done.1, f32[160,2,1]{2,1,0:T(2,128)S(1)} %get-tuple-element.229, f32[160,2,1023]{2,1,0:T(2,128)S(1)} %get-tuple-element.230, ...), kind=kLoop, calls=%fused_computation.4.clone.1 | loop fusion | flops 4259840 | bytes 6594560 | tf_op jit(solution)/shard_map/while/body/eval_jaxpr/add | solution.py:46
  86.5 12.1 %collective-permute-start.1 = (f32[160,1,1024]{2,1,0:T(1,128)S(1)}, f32[160,1,1024]{2,1,0:T(1,128)}, u32[]{:S(2)}, u32[]{:S(2)}) collective-permute-start(f32[160,1,1024]{2,1,0:T(1,128)S(1)} %get-tuple-element.228), channel_id=1, source_target_pairs={{0,1},{1,2},{2,3},{3,4},{4,5},{5,6},{6,7},{7,8},{8,9},{9,10},{10,1... | collective-permute-start | bytes 1966088 | tf_op jit(solution)/shard_map/while/body/eval_jaxpr/ppermute | solution.py:18
  101.4 1.8 fusion.73
  103.2 5.9 %fusion.74 = f32[160,2,1024]{2,1,0:T(2,128)S(1)} fusion(f32[160,1,1024]{2,1,0:T(1,128)S(1)} %collective-permute-done, f32[160,2,1024]{2,1,0:T(2,128)S(1)} %copy.37, f32[160,1,1024]{2,1,0:T(1,128)} %collective-permute-done.1, f32[160,2,1]{2,1,0:T(2,128)S(1)} %get-tuple-element.229, f32[160,2,1023]{2,1,0:T(2,128)S(1)} %get-tuple-element.230, ...), kind=kLoop, calls=%fused_computation.4.clone.1 | loop fusion | flops 4259840 | bytes 6594560 | tf_op jit(solution)/shard_map/while/body/eval_jaxpr/add | solution.py:46
  111.9 1.8 fusion.30
  118.3 96.1 %while.21 = (s32[]{:T(128)}, f32[160,2,1024]{2,1,0:T(2,128)S(1)}, f32[4,1024]{1,0:T(4,128)}, f32[4,1024]{1,0:T(4,128)}, f32[4,1024]{1,0:T(4,128)}, /*index=5*/f32[4,1024]{1,0:T(4,128)}, f32[4,1024]{1,0:T(4,128)}, s32[]{:T(128)}) while((s32[]{:T(128)}, f32[160,2,1024]{2,1,0:T(2,128)S(1)}, f32[4,1024]{1,0:T(4,128)}, f32[4,1024]{1,0:T(4,128)}, ...), condition=%wide.region_3.4_spmd, body=%wide.region_2.3_spmd.sunk | while | flops 4259842 | bytes 22864288 | solution.py:61
  121.4 9.1 %collective-permute-start.3 = (f32[160,1,1024]{2,1,0:T(1,128)S(1)}, f32[160,1,1024]{2,1,0:T(1,128)}, u32[]{:S(2)}, u32[]{:S(2)}) collective-permute-start(f32[160,1,1024]{2,1,0:T(1,128)S(1)} %get-tuple-element.241), channel_id=1, source_target_pairs={{0,1},{1,2},{2,3},{3,4},{4,5},{5,6},{6,7},{7,8},{8,9},{9,10},{10,1... | collective-permute-start | bytes 1966088 | tf_op jit(solution)/shard_map/while/body/eval_jaxpr/ppermute | solution.py:18
  133.2 1.8 fusion.77
  135.1 5.9 %fusion.78 = f32[160,2,1024]{2,1,0:T(2,128)S(1)} fusion(f32[160,1,1024]{2,1,0:T(1,128)S(1)} %collective-permute-done.2, f32[160,2,1024]{2,1,0:T(2,128)S(1)} %copy.38, f32[160,1,1024]{2,1,0:T(1,128)} %collective-permute-done.3, f32[160,2,1]{2,1,0:T(2,128)S(1)} %get-tuple-element.242, f32[160,2,1023]{2,1,0:T(2,128)S(1)} %get-tuple-element.243, ...), kind=kLoop, calls=%fused_computation.14.clone.1 | loop fusion | flops 4259840 | bytes 6594560 | tf_op jit(solution)/shard_map/while/body/eval_jaxpr/add | solution.py:46
  143.9 12.2 %collective-permute-start.3 = (f32[160,1,1024]{2,1,0:T(1,128)S(1)}, f32[160,1,1024]{2,1,0:T(1,128)}, u32[]{:S(2)}, u32[]{:S(2)}) collective-permute-start(f32[160,1,1024]{2,1,0:T(1,128)S(1)} %get-tuple-element.241), channel_id=1, source_target_pairs={{0,1},{1,2},{2,3},{3,4},{4,5},{5,6},{6,7},{7,8},{8,9},{9,10},{10,1... | collective-permute-start | bytes 1966088 | tf_op jit(solution)/shard_map/while/body/eval_jaxpr/ppermute | solution.py:18
  158.7 1.8 fusion.77
  160.6 5.9 %fusion.78 = f32[160,2,1024]{2,1,0:T(2,128)S(1)} fusion(f32[160,1,1024]{2,1,0:T(1,128)S(1)} %collective-permute-done.2, f32[160,2,1024]{2,1,0:T(2,128)S(1)} %copy.38, f32[160,1,1024]{2,1,0:T(1,128)} %collective-permute-done.3, f32[160,2,1]{2,1,0:T(2,128)S(1)} %get-tuple-element.242, f32[160,2,1023]{2,1,0:T(2,128)S(1)} %get-tuple-element.243, ...), kind=kLoop, calls=%fused_computation.14.clone.1 | loop fusion | flops 4259840 | bytes 6594560 | tf_op jit(solution)/shard_map/while/body/eval_jaxpr/add | solution.py:46
  169.4 9.2 %collective-permute-start.3 = (f32[160,1,1024]{2,1,0:T(1,128)S(1)}, f32[160,1,1024]{2,1,0:T(1,128)}, u32[]{:S(2)}, u32[]{:S(2)}) collective-permute-start(f32[160,1,1024]{2,1,0:T(1,128)S(1)} %get-tuple-element.241), channel_id=1, source_target_pairs={{0,1},{1,2},{2,3},{3,4},{4,5},{5,6},{6,7},{7,8},{8,9},{9,10},{10,1... | collective-permute-start | bytes 1966088 | tf_op jit(solution)/shard_map/while/body/eval_jaxpr/ppermute | solution.py:18
  183.1 5.9 %fusion.78 = f32[160,2,1024]{2,1,0:T(2,128)S(1)} fusion(f32[160,1,1024]{2,1,0:T(1,128)S(1)} %collective-permute-done.2, f32[160,2,1024]{2,1,0:T(2,128)S(1)} %copy.38, f32[160,1,1024]{2,1,0:T(1,128)} %collective-permute-done.3, f32[160,2,1]{2,1,0:T(2,128)S(1)} %get-tuple-element.242, f32[160,2,1023]{2,1,0:T(2,128)S(1)} %get-tuple-element.243, ...), kind=kLoop, calls=%fused_computation.14.clone.1 | loop fusion | flops 4259840 | bytes 6594560 | tf_op jit(solution)/shard_map/while/body/eval_jaxpr/add | solution.py:46
  191.9 12.0 %collective-permute-start.3 = (f32[160,1,1024]{2,1,0:T(1,128)S(1)}, f32[160,1,1024]{2,1,0:T(1,128)}, u32[]{:S(2)}, u32[]{:S(2)}) collective-permute-start(f32[160,1,1024]{2,1,0:T(1,128)S(1)} %get-tuple-element.241), channel_id=1, source_target_pairs={{0,1},{1,2},{2,3},{3,4},{4,5},{5,6},{6,7},{7,8},{8,9},{9,10},{10,1... | collective-permute-start | bytes 1966088 | tf_op jit(solution)/shard_map/while/body/eval_jaxpr/ppermute | solution.py:18
  206.7 1.8 fusion.77
  208.5 5.9 %fusion.78 = f32[160,2,1024]{2,1,0:T(2,128)S(1)} fusion(f32[160,1,1024]{2,1,0:T(1,128)S(1)} %collective-permute-done.2, f32[160,2,1024]{2,1,0:T(2,128)S(1)} %copy.38, f32[160,1,1024]{2,1,0:T(1,128)} %collective-permute-done.3, f32[160,2,1]{2,1,0:T(2,128)S(1)} %get-tuple-element.242, f32[160,2,1023]{2,1,0:T(2,128)S(1)} %get-tuple-element.243, ...), kind=kLoop, calls=%fused_computation.14.clone.1 | loop fusion | flops 4259840 | bytes 6594560 | tf_op jit(solution)/shard_map/while/body/eval_jaxpr/add | solution.py:46
  221.2 36.8 %all-gather.3 = f32[16,16,6]{1,2,0:T(8,128)S(1)} all-gather(f32[1,16,6]{1,2,0:T(8,128)S(1)} %convolution_bitcast_fusion.2), channel_id=3, replica_groups=mesh['ens'=2,'tile'=16] {'tile'}, dimensions={0}, use_global_device_ids=true | all-gather | bytes 6528 | tf_op jit(solution)/shard_map/all_gather | solution.py:115
  260.8 17.6 %all-gather.2 = f32[16,16,6]{1,2,0:T(8,128)S(1)} all-gather(f32[1,16,6]{1,2,0:T(8,128)S(1)} %convolution_bitcast_fusion.3), channel_id=2, replica_groups=mesh['ens'=2,'tile'=16] {'tile'}, dimensions={0}, use_global_device_ids=true | all-gather | bytes 6528 | tf_op jit(solution)/shard_map/all_gather | solution.py:115
  278.6 2.2 reshape.64
  (322 shorter events, 69.9 us)
Async XLA Ops:
  1.4 12.3 %collective-permute-start.4 = (f32[3,2,1024]{2,1,0:T(2,128)S(1)}, f32[3,2,1024]{2,1,0:T(2,128)S(1)}, u32[]{:S(2)}, u32[]{:S(2)}) collective-permute-start(f32[3,2,1024]{2,1,0:T(2,128)S(1)} %pad_maximum_fusion.7), channel_id=1, source_target_pairs={{0,1},{1,2},{2,3},{3,4},{4,5},{5,6},{6,7},{7,8},{8,9},{9,10},{10,1... | collective-permute-start | bytes 73736 | tf_op jit(solution)/shard_map/ppermute | solution.py:18
  3.8 9.9 %collective-permute-start.5 = (f32[3,2,1024]{2,1,0:T(2,128)S(1)}, f32[3,2,1024]{2,1,0:T(2,128)S(1)}, u32[]{:S(2)}, u32[]{:S(2)}) collective-permute-start(f32[3,2,1024]{2,1,0:T(2,128)S(1)} %pad_maximum_fusion.7), channel_id=1, source_target_pairs={{1,0},{2,1},{3,2},{4,3},{5,4},{6,5},{7,6},{8,7},{9,8},{10,9},{11,1... | collective-permute-start | bytes 73736 | tf_op jit(solution)/shard_map/ppermute | solution.py:20
  16.1 12.4 %collective-permute-start = (f32[160,1,1024]{2,1,0:T(1,128)S(1)}, f32[160,1,1024]{2,1,0:T(1,128)S(1)}, u32[]{:S(2)}, u32[]{:S(2)}) collective-permute-start(f32[160,1,1024]{2,1,0:T(1,128)S(1)} %get-tuple-element.227), channel_id=1, source_target_pairs={{1,0},{2,1},{3,2},{4,3},{5,4},{6,5},{7,6},{8,7},{9,8},{10,9},{11,1... | collective-permute-start | bytes 1966088 | tf_op jit(solution)/shard_map/while/body/eval_jaxpr/ppermute | solution.py:20
  17.4 11.2 %collective-permute-start.1 = (f32[160,1,1024]{2,1,0:T(1,128)S(1)}, f32[160,1,1024]{2,1,0:T(1,128)}, u32[]{:S(2)}, u32[]{:S(2)}) collective-permute-start(f32[160,1,1024]{2,1,0:T(1,128)S(1)} %get-tuple-element.228), channel_id=1, source_target_pairs={{0,1},{1,2},{2,3},{3,4},{4,5},{5,6},{6,7},{7,8},{8,9},{9,10},{10,1... | collective-permute-start | bytes 1966088 | tf_op jit(solution)/shard_map/while/body/eval_jaxpr/ppermute | solution.py:18
  35.0 15.7 %copy-start.32 = (f32[4,1024]{1,0:T(4,128)S(1)}, f32[4,1024]{1,0:T(4,128)}, u32[]{:S(2)}) copy-start(f32[4,1024]{1,0:T(4,128)} %get-tuple-element.268) | copy-start | bytes 49156 | tf_op jit(solution)/shard_map/while
  35.0 15.7 %copy-start.30 = (f32[4,1024]{1,0:T(4,128)S(1)}, f32[4,1024]{1,0:T(4,128)}, u32[]{:S(2)}) copy-start(f32[4,1024]{1,0:T(4,128)} %get-tuple-element.267) | copy-start | bytes 49156 | tf_op jit(solution)/shard_map/while
  35.0 16.3 %copy-start.28 = (f32[4,1024]{1,0:T(4,128)S(1)}, f32[4,1024]{1,0:T(4,128)}, u32[]{:S(2)}) copy-start(f32[4,1024]{1,0:T(4,128)} %get-tuple-element.266) | copy-start | bytes 49156 | tf_op jit(solution)/shard_map/while
  35.0 16.9 %copy-start.26 = (f32[4,1024]{1,0:T(4,128)S(1)}, f32[4,1024]{1,0:T(4,128)}, u32[]{:S(2)}) copy-start(f32[4,1024]{1,0:T(4,128)} %get-tuple-element.265) | copy-start | bytes 49156 | tf_op jit(solution)/shard_map/while
  35.0 17.5 %copy-start.24 = (f32[4,1024]{1,0:T(4,128)S(1)}, f32[4,1024]{1,0:T(4,128)}, u32[]{:S(2)}) copy-start(f32[4,1024]{1,0:T(4,128)} %get-tuple-element.264) | copy-start | bytes 49156 | tf_op jit(solution)/shard_map/while
  36.1 19.1 %collective-permute-start = (f32[160,1,1024]{2,1,0:T(1,128)S(1)}, f32[160,1,1024]{2,1,0:T(1,128)S(1)}, u32[]{:S(2)}, u32[]{:S(2)}) collective-permute-start(f32[160,1,1024]{2,1,0:T(1,128)S(1)} %get-tuple-element.227), channel_id=1, source_target_pairs={{1,0},{2,1},{3,2},{4,3},{5,4},{6,5},{7,6},{8,7},{9,8},{10,9},{11,1... | collective-permute-start | bytes 1966088 | tf_op jit(solution)/shard_map/while/body/eval_jaxpr/ppermute | solution.py:20
  37.4 17.8 %collective-permute-start.1 = (f32[160,1,1024]{2,1,0:T(1,128)S(1)}, f32[160,1,1024]{2,1,0:T(1,128)}, u32[]{:S(2)}, u32[]{:S(2)}) collective-permute-start(f32[160,1,1024]{2,1,0:T(1,128)S(1)} %get-tuple-element.228), channel_id=1, source_target_pairs={{0,1},{1,2},{2,3},{3,4},{4,5},{5,6},{6,7},{7,8},{8,9},{9,10},{10,1... | collective-permute-start | bytes 1966088 | tf_op jit(solution)/shard_map/while/body/eval_jaxpr/ppermute | solution.py:18
  62.7 14.9 %collective-permute-start = (f32[160,1,1024]{2,1,0:T(1,128)S(1)}, f32[160,1,1024]{2,1,0:T(1,128)S(1)}, u32[]{:S(2)}, u32[]{:S(2)}) collective-permute-start(f32[160,1,1024]{2,1,0:T(1,128)S(1)} %get-tuple-element.227), channel_id=1, source_target_pairs={{1,0},{2,1},{3,2},{4,3},{5,4},{6,5},{7,6},{8,7},{9,8},{10,9},{11,1... | collective-permute-start | bytes 1966088 | tf_op jit(solution)/shard_map/while/body/eval_jaxpr/ppermute | solution.py:20
  64.0 13.6 %collective-permute-start.1 = (f32[160,1,1024]{2,1,0:T(1,128)S(1)}, f32[160,1,1024]{2,1,0:T(1,128)}, u32[]{:S(2)}, u32[]{:S(2)}) collective-permute-start(f32[160,1,1024]{2,1,0:T(1,128)S(1)} %get-tuple-element.228), channel_id=1, source_target_pairs={{0,1},{1,2},{2,3},{3,4},{4,5},{5,6},{6,7},{7,8},{8,9},{9,10},{10,1... | collective-permute-start | bytes 1966088 | tf_op jit(solution)/shard_map/while/body/eval_jaxpr/ppermute | solution.py:18
  84.2 15.1 %copy-start.28 = (f32[4,1024]{1,0:T(4,128)S(1)}, f32[4,1024]{1,0:T(4,128)}, u32[]{:S(2)}) copy-start(f32[4,1024]{1,0:T(4,128)} %get-tuple-element.266) | copy-start | bytes 49156 | tf_op jit(solution)/shard_map/while
  84.2 15.7 %copy-start.26 = (f32[4,1024]{1,0:T(4,128)S(1)}, f32[4,1024]{1,0:T(4,128)}, u32[]{:S(2)}) copy-start(f32[4,1024]{1,0:T(4,128)} %get-tuple-element.265) | copy-start | bytes 49156 | tf_op jit(solution)/shard_map/while
  84.2 16.3 %copy-start.24 = (f32[4,1024]{1,0:T(4,128)S(1)}, f32[4,1024]{1,0:T(4,128)}, u32[]{:S(2)}) copy-start(f32[4,1024]{1,0:T(4,128)} %get-tuple-element.264) | copy-start | bytes 49156 | tf_op jit(solution)/shard_map/while
  85.2 17.9 %collective-permute-start = (f32[160,1,1024]{2,1,0:T(1,128)S(1)}, f32[160,1,1024]{2,1,0:T(1,128)S(1)}, u32[]{:S(2)}, u32[]{:S(2)}) collective-permute-start(f32[160,1,1024]{2,1,0:T(1,128)S(1)} %get-tuple-element.227), channel_id=1, source_target_pairs={{1,0},{2,1},{3,2},{4,3},{5,4},{6,5},{7,6},{8,7},{9,8},{10,9},{11,1... | collective-permute-start | bytes 1966088 | tf_op jit(solution)/shard_map/while/body/eval_jaxpr/ppermute | solution.py:20
  86.5 16.7 %collective-permute-start.1 = (f32[160,1,1024]{2,1,0:T(1,128)S(1)}, f32[160,1,1024]{2,1,0:T(1,128)}, u32[]{:S(2)}, u32[]{:S(2)}) collective-permute-start(f32[160,1,1024]{2,1,0:T(1,128)S(1)} %get-tuple-element.228), channel_id=1, source_target_pairs={{0,1},{1,2},{2,3},{3,4},{4,5},{5,6},{6,7},{7,8},{8,9},{9,10},{10,1... | collective-permute-start | bytes 1966088 | tf_op jit(solution)/shard_map/while/body/eval_jaxpr/ppermute | solution.py:18
  120.1 14.9 %collective-permute-start.2 = (f32[160,1,1024]{2,1,0:T(1,128)S(1)}, f32[160,1,1024]{2,1,0:T(1,128)S(1)}, u32[]{:S(2)}, u32[]{:S(2)}) collective-permute-start(f32[160,1,1024]{2,1,0:T(1,128)S(1)} %get-tuple-element.240), channel_id=1, source_target_pairs={{1,0},{2,1},{3,2},{4,3},{5,4},{6,5},{7,6},{8,7},{9,8},{10,9},{11,1... | collective-permute-start | bytes 1966088 | tf_op jit(solution)/shard_map/while/body/eval_jaxpr/ppermute | solution.py:20
  121.4 13.6 %collective-permute-start.3 = (f32[160,1,1024]{2,1,0:T(1,128)S(1)}, f32[160,1,1024]{2,1,0:T(1,128)}, u32[]{:S(2)}, u32[]{:S(2)}) collective-permute-start(f32[160,1,1024]{2,1,0:T(1,128)S(1)} %get-tuple-element.241), channel_id=1, source_target_pairs={{0,1},{1,2},{2,3},{3,4},{4,5},{5,6},{6,7},{7,8},{8,9},{9,10},{10,1... | collective-permute-start | bytes 1966088 | tf_op jit(solution)/shard_map/while/body/eval_jaxpr/ppermute | solution.py:18
  141.5 15.1 %copy-start.29 = (f32[4,1024]{1,0:T(4,128)S(1)}, f32[4,1024]{1,0:T(4,128)}, u32[]{:S(2)}) copy-start(f32[4,1024]{1,0:T(4,128)} %get-tuple-element.290) | copy-start | bytes 49156 | tf_op jit(solution)/shard_map/while
  141.5 15.7 %copy-start.27 = (f32[4,1024]{1,0:T(4,128)S(1)}, f32[4,1024]{1,0:T(4,128)}, u32[]{:S(2)}) copy-start(f32[4,1024]{1,0:T(4,128)} %get-tuple-element.289) | copy-start | bytes 49156 | tf_op jit(solution)/shard_map/while
  141.5 16.3 %copy-start.25 = (f32[4,1024]{1,0:T(4,128)S(1)}, f32[4,1024]{1,0:T(4,128)}, u32[]{:S(2)}) copy-start(f32[4,1024]{1,0:T(4,128)} %get-tuple-element.288) | copy-start | bytes 49156 | tf_op jit(solution)/shard_map/while
  142.6 17.9 %collective-permute-start.2 = (f32[160,1,1024]{2,1,0:T(1,128)S(1)}, f32[160,1,1024]{2,1,0:T(1,128)S(1)}, u32[]{:S(2)}, u32[]{:S(2)}) collective-permute-start(f32[160,1,1024]{2,1,0:T(1,128)S(1)} %get-tuple-element.240), channel_id=1, source_target_pairs={{1,0},{2,1},{3,2},{4,3},{5,4},{6,5},{7,6},{8,7},{9,8},{10,9},{11,1... | collective-permute-start | bytes 1966088 | tf_op jit(solution)/shard_map/while/body/eval_jaxpr/ppermute | solution.py:20
  143.9 16.7 %collective-permute-start.3 = (f32[160,1,1024]{2,1,0:T(1,128)S(1)}, f32[160,1,1024]{2,1,0:T(1,128)}, u32[]{:S(2)}, u32[]{:S(2)}) collective-permute-start(f32[160,1,1024]{2,1,0:T(1,128)S(1)} %get-tuple-element.241), channel_id=1, source_target_pairs={{0,1},{1,2},{2,3},{3,4},{4,5},{5,6},{6,7},{7,8},{8,9},{9,10},{10,1... | collective-permute-start | bytes 1966088 | tf_op jit(solution)/shard_map/while/body/eval_jaxpr/ppermute | solution.py:18
  168.1 15.0 %collective-permute-start.2 = (f32[160,1,1024]{2,1,0:T(1,128)S(1)}, f32[160,1,1024]{2,1,0:T(1,128)S(1)}, u32[]{:S(2)}, u32[]{:S(2)}) collective-permute-start(f32[160,1,1024]{2,1,0:T(1,128)S(1)} %get-tuple-element.240), channel_id=1, source_target_pairs={{1,0},{2,1},{3,2},{4,3},{5,4},{6,5},{7,6},{8,7},{9,8},{10,9},{11,1... | collective-permute-start | bytes 1966088 | tf_op jit(solution)/shard_map/while/body/eval_jaxpr/ppermute | solution.py:20
  169.4 13.7 %collective-permute-start.3 = (f32[160,1,1024]{2,1,0:T(1,128)S(1)}, f32[160,1,1024]{2,1,0:T(1,128)}, u32[]{:S(2)}, u32[]{:S(2)}) collective-permute-start(f32[160,1,1024]{2,1,0:T(1,128)S(1)} %get-tuple-element.241), channel_id=1, source_target_pairs={{0,1},{1,2},{2,3},{3,4},{4,5},{5,6},{6,7},{7,8},{8,9},{9,10},{10,1... | collective-permute-start | bytes 1966088 | tf_op jit(solution)/shard_map/while/body/eval_jaxpr/ppermute | solution.py:18
  189.6 15.6 %copy-start.27 = (f32[4,1024]{1,0:T(4,128)S(1)}, f32[4,1024]{1,0:T(4,128)}, u32[]{:S(2)}) copy-start(f32[4,1024]{1,0:T(4,128)} %get-tuple-element.289) | copy-start | bytes 49156 | tf_op jit(solution)/shard_map/while
  189.6 16.2 %copy-start.25 = (f32[4,1024]{1,0:T(4,128)S(1)}, f32[4,1024]{1,0:T(4,128)}, u32[]{:S(2)}) copy-start(f32[4,1024]{1,0:T(4,128)} %get-tuple-element.288) | copy-start | bytes 49156 | tf_op jit(solution)/shard_map/while
  190.6 17.8 %collective-permute-start.2 = (f32[160,1,1024]{2,1,0:T(1,128)S(1)}, f32[160,1,1024]{2,1,0:T(1,128)S(1)}, u32[]{:S(2)}, u32[]{:S(2)}) collective-permute-start(f32[160,1,1024]{2,1,0:T(1,128)S(1)} %get-tuple-element.240), channel_id=1, source_target_pairs={{1,0},{2,1},{3,2},{4,3},{5,4},{6,5},{7,6},{8,7},{9,8},{10,9},{11,1... | collective-permute-start | bytes 1966088 | tf_op jit(solution)/shard_map/while/body/eval_jaxpr/ppermute | solution.py:20
  191.9 16.6 %collective-permute-start.3 = (f32[160,1,1024]{2,1,0:T(1,128)S(1)}, f32[160,1,1024]{2,1,0:T(1,128)}, u32[]{:S(2)}, u32[]{:S(2)}) collective-permute-start(f32[160,1,1024]{2,1,0:T(1,128)S(1)} %get-tuple-element.241), channel_id=1, source_target_pairs={{0,1},{1,2},{2,3},{3,4},{4,5},{5,6},{6,7},{7,8},{8,9},{9,10},{10,1... | collective-permute-start | bytes 1966088 | tf_op jit(solution)/shard_map/while/body/eval_jaxpr/ppermute | solution.py:18
  259.4 19.1 %copy-start.35 = (f32[6,2048]{1,0:T(8,128)S(1)}, f32[6,2048]{1,0:T(8,128)}, u32[]{:S(2)}) copy-start(f32[6,2048]{1,0:T(8,128)} %get-tuple-element.132) | copy-start | bytes 147460
  (82 other events, 436.9 us)
